TPU v7x, 32 devices: a whole 2x2x4 slice. The times are simulated.
32 devices in a mesh: groups: 2 (over x), sect: 8 (over z, y), head: 2 (over core).
Axes of the slice: x: 2, y: 2, z: 4, core: 2. Of those that a mesh axis runs over, the one named last changes fastest.
Arguments:
- queries: bfloat16 [2048, 8192], P(('groups', 'sect'), 'head'), parts along dimension 0, may hold values from -200 to 200
- packed_key_rows: bfloat16 [2048, 512], P(('groups', 'sect'), 'head'), parts along dimension 0, may hold values from -7 to 7
- values: bfloat16 [2048, 512], P(('groups', 'sect'), 'head'), parts along dimension 0, may hold values from -12 to 12
- segments: int32 [2048], P('groups'), parts along dimension 0, may hold values from 0 to 7, never falling along the last dimension, each value on 1 to 512 neighbouring positions
- proj_weight: bfloat16 [8192, 2048], P('head', 'sect'), may hold values from -0.0625 to 0.0625
- residual: bfloat16 [2048, 2048], P(('groups', 'sect', 'head')), parts along dimension 0, may hold values from -2 to 2
- norm_gain: bfloat16 [2048], replicated, may hold values from 0.5 to 1.5
- expert_ids: int32 [2048, 8], P(('groups', 'sect', 'head')), parts along dimension 0, may hold values from 0 to 15, all different within a row; in each aligned block of 64 rows (0 to 63, 64 to 127, ...) at most 48 rows name the same one
- route_weights: float32 [2048, 8], P(('groups', 'sect', 'head')), parts along dimension 0, may hold values from 0.05 to 1
- gate_weight: bfloat16 [16, 2048, 768], P(('sect', 'head')), may hold values from -0.125 to 0.125
- up_weight: bfloat16 [16, 2048, 768], P(('sect', 'head')), may hold values from -0.125 to 0.125
- down_weight: bfloat16 [16, 768, 2048], P(('sect', 'head')), may hold values from -0.21875 to 0.21875
Outputs:
- hidden_mid: bfloat16 [2048, 2048], P(('groups', 'sect', 'head')), parts along dimension 0
- expert_mix: bfloat16 [2048, 2048], P(('groups', 'sect', 'head')), parts along dimension 0
There are 2 independent parts, one for each index of `groups`. A program takes and returns all parts, laid end to end along the dimension named above; an argument that names none is the same for every part. Nothing has to cross between parts.
Inputs may be any that keep to these rules, and one draw needn't show every extreme that they name: `segments`: ids never fall along the rows; each of the 8 prompts has 1 to 512 rows, and one has exactly that many. `expert_ids`: each row names 8 different experts. Within the rows of one device (aligned blocks of 64 rows) no expert is named by more than 48 rows.
All inputs are finite; a program needn't handle non-finite values.
Results may differ from a plain program's by a relative error of at most 0.02.
Values may be sent and summed in bfloat16 or wider, within the bound.
A program may use at most 256 MiB of HBM per device.

v0:
```python
import math
import jax
import jax.numpy as jnp
from jax import lax
from jax.sharding import PartitionSpec as P

HEAD_WIDTH = 128
negative_large = -1e30
norm_eps = 1e-06


def attend(query_groups, packed_key_rows, values, segments, head_size):
    kv_heads = packed_key_rows.shape[1] // head_size
    score_scale = 1.0 / math.sqrt(head_size)
    prepared = []
    initial_state = []
    for query_rows, query_pos in query_groups:
        query_count = query_rows.shape[0]
        query_group_width = query_rows.shape[1] // head_size // kv_heads
        query_tensor_four = query_rows.reshape(query_count, kv_heads, query_group_width, head_size)
        query_seg = jnp.take(segments, query_pos)
        seg_start = jnp.sum((segments[None, :] < query_seg[:, None]).astype(jnp.int32), axis=1)
        prepared.append(
            (query_tensor_four, query_pos, query_seg, jnp.min(seg_start), jnp.max(query_pos))
        )
        initial_state.append(
            (
                jnp.full((query_count, kv_heads, query_group_width), negative_large, jnp.float32),
                jnp.zeros((query_count, kv_heads, query_group_width), jnp.float32),
                jnp.zeros((query_count, kv_heads, query_group_width, head_size), jnp.float32),
            )
        )
    running = tuple(initial_state)
    first_row = jnp.int32(0)
    key_piece = lax.all_gather(packed_key_rows, "sect", axis=0, tiled=True)
    value_piece = lax.all_gather(values, "sect", axis=0, tiled=True)
    piece_len = key_piece.shape[0]
    key_tensor_three = key_piece.reshape(piece_len, kv_heads, head_size)
    value_tensor_three = value_piece.reshape(piece_len, kv_heads, head_size)
    key_pos = jnp.arange(piece_len, dtype=jnp.int32)
    updated = []
    for state, setup in zip(running, prepared):
        query_tensor_four, query_pos, query_seg, lowest, highest = setup
        needed = jnp.logical_and(first_row <= highest, first_row + piece_len - 1 >= lowest)

        def compute(
            current, query_tensor_four=query_tensor_four, query_pos=query_pos, query_seg=query_seg
        ):
            run_max, run_sum, run_acc = current
            scores = (
                jnp.einsum(
                    "rkgd,pkd->rkgp",
                    query_tensor_four,
                    key_tensor_three,
                    preferred_element_type=jnp.float32,
                )
                * score_scale
            )
            allowed = jnp.logical_and(
                segments[None, :] == query_seg[:, None], key_pos[None, :] <= query_pos[:, None]
            )
            allowed = allowed[:, None, None, :]
            block_max = jnp.max(jnp.where(allowed, scores, negative_large), axis=-1)
            new_max = jnp.maximum(run_max, block_max)
            weights = jnp.where(allowed, jnp.exp(scores - new_max[..., None]), 0.0).astype(
                jnp.bfloat16
            )
            new_sum = jnp.sum(weights.astype(jnp.float32), axis=-1)
            new_acc = jnp.einsum(
                "rkgp,pkd->rkgd", weights, value_tensor_three, preferred_element_type=jnp.float32
            )
            return (new_max, new_sum, new_acc)

        updated.append(lax.cond(needed, compute, lambda kept: kept, state))
    final_state = tuple(updated)
    results = []
    for run_max, run_sum, run_acc in final_state:
        attended = run_acc / run_sum[..., None]
        results.append(attended.reshape(attended.shape[0], -1).astype(jnp.bfloat16))
    return results


def shards(
    queries,
    packed_key_rows,
    values,
    segments,
    proj_weight,
    residual,
    norm_gain,
    expert_ids,
    route_weights,
    gate_weight,
    up_weight,
    down_weight,
):
    row_count = queries.shape[0]
    sect_count = lax.axis_size("sect")
    head_count = lax.axis_size("head")
    sect_pos = lax.axis_index("sect")
    local_pos = jnp.arange(row_count, dtype=jnp.int32)
    own_pos = sect_pos * row_count + local_pos
    attended = attend([(queries, own_pos)], packed_key_rows, values, segments, HEAD_WIDTH)[0]
    partial_value = jnp.dot(
        attended,
        lax.all_gather(proj_weight, "sect", axis=1, tiled=True),
        preferred_element_type=jnp.float32,
    )
    projected = lax.psum_scatter(
        partial_value.astype(jnp.bfloat16), "head", scatter_dimension=0, tiled=True
    ).astype(jnp.float32)
    hidden_mid = (residual.astype(jnp.float32) + projected).astype(jnp.bfloat16)
    mid_float = lax.optimization_barrier(hidden_mid).astype(jnp.float32)
    inverse = lax.rsqrt(jnp.mean(mid_float * mid_float, axis=1, keepdims=True) + norm_eps)
    normed = (mid_float * inverse * norm_gain.astype(jnp.float32)[None, :]).astype(jnp.bfloat16)
    moe_rows = residual.shape[0]
    top_count = expert_ids.shape[1]
    experts = sect_count * head_count
    capacity = max(2, 3 * moe_rows * top_count // (2 * experts))
    flat_ids = expert_ids.reshape(-1)
    onehot = (flat_ids[:, None] == jnp.arange(experts, dtype=jnp.int32)[None, :]).astype(jnp.int32)
    slot_rank = jnp.sum((jnp.cumsum(onehot, axis=0) - 1) * onehot, axis=1)
    slot_index = flat_ids * capacity + slot_rank
    sources = jnp.repeat(normed, top_count, axis=0)
    outgoing = (
        jnp.zeros((experts * capacity, normed.shape[1]), jnp.bfloat16).at[slot_index].set(sources)
    )
    parcels = outgoing.reshape(experts, capacity, -1)
    slot_rows = lax.all_to_all(parcels, ("sect", "head"), split_axis=0, concat_axis=0, tiled=True)
    flat_rows = slot_rows.reshape(-1, slot_rows.shape[-1])
    gate_act = jnp.dot(flat_rows, gate_weight[0], preferred_element_type=jnp.float32)
    up_act = jnp.dot(flat_rows, up_weight[0], preferred_element_type=jnp.float32)
    hidden = (jax.nn.silu(gate_act) * up_act).astype(jnp.bfloat16)
    result = jnp.dot(hidden, down_weight[0], preferred_element_type=jnp.float32).astype(
        jnp.bfloat16
    )
    processed = result.reshape(slot_rows.shape)
    returned_rows = lax.all_to_all(
        processed, ("sect", "head"), split_axis=0, concat_axis=0, tiled=True
    )
    returned_flat = returned_rows.reshape(experts * capacity, -1)
    gathered = returned_flat[slot_index].reshape(moe_rows, top_count, -1)
    route_share = route_weights / jnp.sum(route_weights, axis=1, keepdims=True)
    mixture = jnp.sum(route_share[:, :, None] * gathered.astype(jnp.float32), axis=1)
    return (hidden_mid, mixture.astype(jnp.bfloat16))


def solution(mesh):
    placed = (
        P(("groups", "sect"), "head"),
        P(("groups", "sect"), "head"),
        P(("groups", "sect"), "head"),
        P("groups"),
        P("head", "sect"),
        P(("groups", "sect", "head"), None),
        P(),
        P(("groups", "sect", "head"), None),
        P(("groups", "sect", "head"), None),
        P(("sect", "head"), None, None),
        P(("sect", "head"), None, None),
        P(("sect", "head"), None, None),
    )
    return jax.shard_map(
        shards,
        mesh=mesh,
        in_specs=placed,
        out_specs=(P(("groups", "sect", "head"), None), P(("groups", "sect", "head"), None)),
        check_vma=False,
    )
```

profile of v0, /device:TPU:13, one launch (start us, length us, event | category | flops | bytes accessed | tf_op | source)
XLA Modules:
  0.0 462.3 jit_solution(15963046055641040890)
XLA Ops:
  7.2 0.0 copy-start
  7.2 0.0 copy-start.1
  7.2 0.0 copy-start.4
  7.2 0.0 all-gather.2.cloned.1.call-start
  7.2 0.7 all-gather.2.cloned.1.call-update
  7.9 0.0 reduce-scatter.2.cloned.1.call-start
  8.0 1.8 gather_fusion
  9.8 0.6 and_select_fusion.1
  11.1 0.9 convert_reduce_fusion.1
  12.0 0.6 reduce_min.9
  13.3 32.1 %all_gather.9 = bf16[1024,256]{1,0:T(8,128)(2,1)} all-gather(bf16[128,256]{1,0:T(8,128)(2,1)} %param.15), channel_id=1, replica_groups=mesh['groups'=2,'sect'=8,'head'=2] {'sect'}, dimensions={0}, use_global_device_ids=true | all-gather | bytes 589824 | tf_op jit(solution)/shard_map/all_gather | solution.py:35
  45.4 0.0 copy-done.4
  45.4 33.5 %all_gather.10 = bf16[1024,256]{1,0:T(8,128)(2,1)} all-gather(bf16[128,256]{1,0:T(8,128)(2,1)S(1)} %copy-done.4), channel_id=1, replica_groups=mesh['groups'=2,'sect'=8,'head'=2] {'sect'}, dimensions={0}, use_global_device_ids=true | all-gather | bytes 589824 | tf_op jit(solution)/shard_map/all_gather | solution.py:36
  78.8 0.0 copy-done.1
  78.9 40.8 %conditional.1 = (f32[128,2,16]{0,2,1:T(8,128)S(1)}, f32[128,2,16,128]{0,3,2,1:T(8,128)}) conditional(s32[]{:T(128)} %convert_element_type.61, () %tuple.16, (s32[1024]{0:T(1024)S(1)}, s32[128]{0:T(128)S(1)}, s32[128]{0:T(128)S(1)}, s32[128]{0:T(128)S(1)}, s32[1024]{0:T(1024)S(1)}, /*index=5*/s32[128]{0:T(128)S(1)}, bf16[1024,256]{1,0:T(8,128)(2,1)}, ...), branch_computations={%region_3.4_spmd, %region_4.0_spmd} | conditional | flops 2202399232 | bytes 63548432 | solution.py:74
  78.9 0.3 compare_and_fusion
  79.2 2.4 copy.61
  81.7 2.0 reshape.167
  83.6 9.8 %fusion = (f32[128,2,16]{0,2,1:T(8,128)S(1)}, f32[2,1024,128,16]{2,1,3,0:T(8,128)}) fusion(pred[128,1024]{0,1:T(8,128)(4,1)S(1)} %compare_and_fusion, bf16[128,2,16,128]{3,2,1,0:T(8,128)(2,1)} %bitcast.70, bf16[1024,2,128,1]{2,1,0,3:T(2,128)(2,1)} %bitcast.74), kind=kOutput, calls=%fused_computation.5 | convolution fusion | flops 1086320640 | bytes 18497536 | tf_op jit(solution)/shard_map/cond/branch_1_fun/rkgd,pkd->rkgp/dot_general | solution.py:51
  93.4 9.2 %convert_reduce_fusion = f32[128,2,16]{0,2,1:T(8,128)S(1)} fusion(f32[128,2,16]{0,2,1:T(8,128)S(1)} %broadcast_maximum_fusion, f32[2,1024,128,16]{2,1,3,0:T(8,128)} %get-tuple-element.49, pred[128,1024]{0,1:T(8,128)(4,1)S(1)} %compare_and_fusion), kind=kLoop, calls=%fused_computation.9 | loop fusion | flops 25161728 | bytes 16941056 | tf_op jit(solution)/shard_map/cond/branch_1_fun/reduce_sum | solution.py:68
  102.6 2.0 reshape.169
  104.6 12.1 %convolution_bitcast_fusion = f32[128,2,16,128]{3,0,2,1:T(8,128)} fusion(bf16[1024,2,128,1]{2,1,0,3:T(2,128)(2,1)} %bitcast.76, f32[2,1024,128,16]{2,1,3,0:T(8,128)} %get-tuple-element.49, f32[128,2,16]{0,2,1:T(8,128)S(1)} %broadcast_maximum_fusion, pred[128,1024]{0,1:T(8,128)(4,1)S(1)} %compare_and_fusion), kind=kOutput, calls=%fused_computation.10 | convolution fusion | flops 1090519040 | bytes 19546112 | tf_op jit(solution)/shard_map/cond/branch_1_fun/rkgp,pkd->rkgd/dot_general | solution.py:69
  116.7 3.0 copy.60
  119.7 2.9 divide_convert_fusion
  122.6 125.6 %all-gather.2.cloned.1.call-done = bf16[4096,2048]{1,0:T(8,128)(2,1)} async-done(((bf16[4096,256]{1,0:T(8,128)(2,1)}), bf16[4096,2048]{1,0:T(8,128)(2,1)}) %all-gather.2.cloned.1.call-update) | async-done | bytes 16777232 | tf_op jit(solution)/shard_map/all_gather | solution.py:106
  248.2 0.0 copy-start.5
  248.2 0.0 copy-start.7
  248.2 9.3 %convolution_convert_fusion.1 = bf16[128,2048]{1,0:T(8,128)(2,1)} fusion(bf16[128,4096]{0,1:T(8,128)(2,1)} %bitcast.69, bf16[4096,2048]{1,0:T(8,128)(2,1)} %all-gather.2.cloned.1.call-done), kind=kOutput, calls=%fused_computation.28 | convolution fusion | flops 2147745792 | bytes 18350080 | tf_op jit(solution)/shard_map/dot_general | solution.py:104
  257.5 0.0 reduce-scatter.2.cloned.1.call-update
  257.5 0.0 copy-done.5
  257.5 0.1 copy.49
  257.6 0.1 eq.42
  257.7 0.1 eq.46
  257.8 0.1 copy.48
  257.9 0.1 mul.66
  258.0 1.2 reduce-window.6
  259.1 0.2 slice_reduce_fusion
  259.4 0.0 copy-done.7
  259.4 0.1 fusion.29
  259.5 8.3 %reduce-scatter.2.cloned.1.call-done = bf16[64,2048]{1,0:T(8,128)(2,1)} async-done(((bf16[128,2048]{1,0:T(8,128)(2,1)}), bf16[64,2048]{1,0:T(8,128)(2,1)}) %reduce-scatter.2.cloned.1.call-update) | async-done | bytes 262160 | tf_op jit(solution)/shard_map/reduce_scatter | solution.py:109
  267.8 1.1 add_convert_fusion
  268.9 0.0 copy-start.3
  268.9 0.2 fusion.25
  269.0 0.8 fusion.27
  269.9 6.1 %scatter_custom_fusion = bf16[768,2048]{1,0:T(8,128)(2,1)} fusion(s32[512]{0:T(512)S(1)} %bitcast.77, bf16[]{:T(256)} %constant.60.clone.1, bf16[64,2048]{1,0:T(8,128)(2,1)} %fusion.27), kind=kCustom, calls=%fused_computation.30 | custom fusion | bytes 3407874 | tf_op jit(solution)/shard_map/scatter | solution.py:126
  276.0 0.0 copy-start.8
  276.0 75.8 %all_to_all.10 = bf16[16,48,2048]{2,1,0:T(8,128)(2,1)S(1)} all-to-all(bf16[16,48,2048]{2,1,0:T(8,128)(2,1)} %bitcast.68), channel_id=1, replica_groups=mesh['groups'=2,'sect'=8,'head'=2] {'sect','head'}, dimensions={0} | all-to-all | bytes 6291456 | tf_op jit(solution)/shard_map/all_to_all | solution.py:129
  351.8 0.0 copy-done.3
  351.8 0.0 copy-start.2
  351.8 1.7 copy-done.2
  353.5 0.0 copy-done.8
  353.5 4.0 fusion.13
  357.5 0.0 copy-done
  357.5 11.0 %convolution_convert_fusion = bf16[768,2048]{1,0:T(8,128)(2,1)} fusion(bf16[1,768,2048]{2,1,0:T(8,128)(2,1)S(1)} %copy-done, f32[768,768]{1,0:T(8,128)} %fusion.13, bf16[768,2048]{1,0:T(8,128)(2,1)} %bitcast.73, bf16[1,2048,768]{2,1,0:T(8,128)(2,1)} %param.23), kind=kOutput, calls=%fused_computation.22 | convolution fusion | flops 4836950016 | bytes 14942208 | tf_op jit(solution)/shard_map/dot_general | solution.py:134
  368.5 0.0 copy-start.6
  368.5 5.2 %all-to-all-start.1 = ((bf16[16,48,2048]{2,1,0:T(8,128)(2,1)}), bf16[16,48,2048]{2,1,0:T(8,128)(2,1)}, u32[]{:S(2)}, u32[]{:S(2)}) async-start(bf16[16,48,2048]{2,1,0:T(8,128)(2,1)} %bitcast.71), calls=%async_computation.2 | async-start | bytes 6291456 | tf_op jit(solution)/shard_map/all_to_all | solution.py:138
  373.7 0.0 copy-done.6
  373.8 0.1 copy.47
  373.9 69.9 %all-to-all-done.1 = bf16[16,48,2048]{2,1,0:T(8,128)(2,1)} async-done(((bf16[16,48,2048]{2,1,0:T(8,128)(2,1)}), bf16[16,48,2048]{2,1,0:T(8,128)(2,1)}, u32[]{:S(2)}, u32[]{:S(2)}) %all-to-all-start.1) | async-done | bytes 3145760 | tf_op jit(solution)/shard_map/all_to_all | solution.py:138
  443.7 7.6 %gather_fusion.1 = bf16[512,2048]{1,0:T(8,128)(2,1)} fusion(bf16[768,2048]{1,0:T(8,128)(2,1)} %bitcast.16, s32[1024]{0:T(1024)S(1)} %pad_clamp_fusion), kind=kCustom, calls=%fused_computation.1 | custom fusion | bytes 4196352 | tf_op jit(solution)/shard_map/gather | solution.py:142
  451.3 4.1 fusion.11
  (17 shorter events, 0.1 us)
Async XLA Ops:
  7.2 350.4 %copy-start = (bf16[1,768,2048]{2,1,0:T(8,128)(2,1)S(1)}, bf16[1,768,2048]{2,1,0:T(8,128)(2,1)}, u32[]{:S(2)}) copy-start(bf16[1,768,2048]{2,1,0:T(8,128)(2,1)} %param.25) | copy-start | bytes 9437188
  7.2 71.7 %copy-start.1 = (s32[1024]{0:T(1024)S(1)}, s32[1024]{0:T(1024)}, u32[]{:S(2)}) copy-start(s32[1024]{0:T(1024)} %param.17) | copy-start | bytes 12292
  7.2 38.2 %copy-start.4 = (bf16[128,256]{1,0:T(8,128)(2,1)S(1)}, bf16[128,256]{1,0:T(8,128)(2,1)}, u32[]{:S(2)}) copy-start(bf16[128,256]{1,0:T(8,128)(2,1)} %param.16) | copy-start | bytes 196612
  7.2 241.0 %all-gather.2.cloned.1.call-start = ((), (), s32[]{:S(2)}) async-start(), calls=%async_computation.3 | async-start | bytes 18874368 | tf_op jit(solution)/shard_map/all_gather | solution.py:106
  7.9 259.8 %reduce-scatter.2.cloned.1.call-start = ((), (), s32[]{:S(2)}) async-start(), calls=%async_computation.4 | async-start | bytes 786432 | tf_op jit(solution)/shard_map/reduce_scatter | solution.py:109
  248.2 9.3 %copy-start.5 = (s32[64,8]{0,1:T(8,128)S(1)}, s32[64,8]{0,1:T(8,128)}, u32[]{:S(2)}) copy-start(s32[64,8]{0,1:T(8,128)} %param.21) | copy-start | bytes 6148
  248.2 11.2 %copy-start.7 = (bf16[2048]{0:T(1024)(128)(2,1)S(1)}, bf16[2048]{0:T(1024)(128)(2,1)}, u32[]{:S(2)}) copy-start(bf16[2048]{0:T(1024)(128)(2,1)} %param.20) | copy-start | bytes 12292
  268.9 82.9 %copy-start.3 = (bf16[64,2048]{1,0:T(8,128)(2,1)}, bf16[64,2048]{1,0:T(8,128)(2,1)S(1)}, u32[]{:S(2)}) copy-start(bf16[64,2048]{1,0:T(8,128)(2,1)S(1)} %add_convert_fusion) | copy-start | bytes 786436
  276.0 77.5 %copy-start.8 = (bf16[1,2048,768]{2,1,0:T(8,128)(2,1)S(1)}, bf16[1,2048,768]{2,1,0:T(8,128)(2,1)}, u32[]{:S(2)}) copy-start(bf16[1,2048,768]{2,1,0:T(8,128)(2,1)} %param.24) | copy-start | bytes 9437188
  351.8 1.7 copy-start.2
  368.5 5.2 %copy-start.6 = (f32[64,8]{0,1:T(8,128)S(1)}, f32[64,8]{0,1:T(8,128)}, u32[]{:S(2)}) copy-start(f32[64,8]{0,1:T(8,128)} %param.22) | copy-start | bytes 6148
  368.5 75.2 %all-to-all-start.1 = ((bf16[16,48,2048]{2,1,0:T(8,128)(2,1)}), bf16[16,48,2048]{2,1,0:T(8,128)(2,1)}, u32[]{:S(2)}, u32[]{:S(2)}) async-start(bf16[16,48,2048]{2,1,0:T(8,128)(2,1)} %bitcast.71), calls=%async_computation.2 | async-start | bytes 6291456 | tf_op jit(solution)/shard_map/all_to_all | solution.py:138
Sparse Core Ops, SparseCore 0:
  10.1 238.0 all-gather.1
  257.6 10.1 reduce-scatter.1
where the time goes:
time: 463 us; the launch traced here: 462 us
  waiting for transfers between devices  204 us (44%)
  blocking collectives  141 us (30%)
  matrix products  46.1 us (10%)
  local copies, waits for them, and re-layouts  27.3 us (6%)
  other arithmetic  22.3 us (5%)
  between operations  15.5 us (3%)
  starting transfers between devices  5.31 us (1%)
    all_gather x1, waiting for transfers between devices, shards(): lax.all_gather(proj_weight, 'sect', axis=1, tiled=True)  126 us
    all_to_all x1, blocking collectives, shards(): lax.all_to_all(parcels, ('sect', 'head'), split_axis=0, concat_axis=0, ti...  75.8 us
    all_to_all x1, waiting for transfers between devices, shards(): lax.all_to_all(processed, ('sect', 'head'), split_axis=0, concat_axis=0,...  69.9 us
    all_gather x1, blocking collectives, attend(): value_piece = lax.all_gather(values, 'sect', axis=0, tiled=True)  33.5 us
    all_gather x1, blocking collectives, attend(): key_piece = lax.all_gather(packed_key_rows, 'sect', axis=0, tiled=True)  32.1 us
    dot_general x1, matrix products, compute(): jnp.einsum('rkgp,pkd->rkgd', weights, value_tensor_three, preferred_eleme...  12.1 us
    dot_general x1, matrix products, shards(): jnp.dot(hidden, down_weight[0], preferred_element_type=jnp.float32)  11 us
    dot_general x1, matrix products, compute(): jnp.einsum('rkgd,pkd->rkgp', query_tensor_four, key_tensor_three, preferr...  9.76 us
  transfers between devices with their start and end apart: 3, of which 3 were waited for; matrix products, arithmetic and copies ran while one was open for 11% of the time, Pallas kernels for 0%

commit v1 on v0

--- a/solution.py
+++ b/solution.py
@@ -32,8 +32,13 @@
         )
     running = tuple(initial_state)
     first_row = jnp.int32(0)
-    key_piece = lax.all_gather(packed_key_rows, "sect", axis=0, tiled=True)
-    value_piece = lax.all_gather(values, "sect", axis=0, tiled=True)
+    key_piece, value_piece = jnp.split(
+        lax.all_gather(
+            jnp.concatenate([packed_key_rows, values], axis=1), "sect", axis=0, tiled=True
+        ),
+        [packed_key_rows.shape[1]],
+        axis=1,
+    )
     piece_len = key_piece.shape[0]
     key_tensor_three = key_piece.reshape(piece_len, kv_heads, head_size)
     value_tensor_three = value_piece.reshape(piece_len, kv_heads, head_size)

time: 463 us -> 491 us (1.060)
  waiting for transfers between devices: 204 us -> 300 us
  blocking collectives: 141 us -> 75.8 us
    all_gather x2 -> x0, blocking collectives: 65.6 us -> none  [the longest x1 33.5 us: attend(): value_piece = lax.all_gather(values, 'sect', axis=0, tiled=True)]
    all_gather x1, waiting for transfers between devices: 126 us -> 187 us  [shards(): lax.all_gather(proj_weight, 'sect', axis=1, tiled=True)]
    all_gather x0 -> x1, waiting for transfers between devices: none -> 33.7 us  [attend(): lax.all_gather(jnp.concatenate([packed_key_rows, values], axis=1), 'sect'...]
  transfers between devices with their start and end apart: 3 -> 4, of which waited for: 3 -> 4; matrix products, arithmetic and copies ran while one was open for 11% -> 9% of each run, Pallas kernels for 0% -> 0%
where the time goes in v1:
time: 491 us; the launch traced here: 490 us
  waiting for transfers between devices  300 us (61%)
  blocking collectives  75.8 us (15%)
  matrix products  43.8 us (9%)
  local copies, waits for them, and re-layouts  26.3 us (5%)
  other arithmetic  23.6 us (5%)
  between operations  15.2 us (3%)
  starting transfers between devices  5.35 us (1%)
    all_gather x1, waiting for transfers between devices, shards(): lax.all_gather(proj_weight, 'sect', axis=1, tiled=True)  187 us
    all_to_all x1, blocking collectives, shards(): lax.all_to_all(parcels, ('sect', 'head'), split_axis=0, concat_axis=0, ti...  75.8 us
    all_to_all x1, waiting for transfers between devices, shards(): lax.all_to_all(processed, ('sect', 'head'), split_axis=0, concat_axis=0,...  69.9 us
    all_gather x1, waiting for transfers between devices, attend(): lax.all_gather(jnp.concatenate([packed_key_rows, values], axis=1), 'sect'...  33.7 us
    dot_general x1, matrix products, compute(): jnp.einsum('rkgp,pkd->rkgd', weights, value_tensor_three, preferred_eleme...  12 us
    dot_general x1, matrix products, shards(): jnp.dot(hidden, down_weight[0], preferred_element_type=jnp.float32)  11 us
    reduce_sum x1, other arithmetic, compute(): new_sum = jnp.sum(weights.astype(jnp.float32), axis=-1)  10.6 us
  transfers between devices with their start and end apart: 4, of which 4 were waited for; matrix products, arithmetic and copies ran while one was open for 9% of the time, Pallas kernels for 0%

profile of v1, /device:TPU:13, one launch (start us, length us, event | category | flops | bytes accessed | tf_op | source)
XLA Modules:
  0.0 490.1 jit_solution(7620530907223635590)
XLA Ops:
  7.2 0.0 copy-start
  7.2 0.0 copy-start.1
  7.2 0.0 all-gather.3.cloned.1.call-start
  7.2 1.1 copy.49
  8.3 1.0 copy.48
  9.3 0.7 pad_maximum_fusion
  10.0 0.0 all-gather.3.cloned.1.call-update
  10.0 0.0 all-gather.5.cloned.1.call-start
  10.1 0.7 all-gather.5.cloned.1.call-update
  10.8 0.0 reduce-scatter.2.cloned.1.call-start
  10.8 1.6 gather_fusion
  12.5 0.6 and_select_fusion.1
  13.7 0.0 copy-done.1
  13.8 0.2 convert_reduce_fusion.1
  14.0 0.6 reduce_min.9
  15.3 33.7 %all-gather.3.cloned.1.call-done = bf16[1024,512]{0,1:T(8,128)(2,1)} async-done(((bf16[128,512]{0,1:T(8,128)(2,1)}), bf16[1024,512]{0,1:T(8,128)(2,1)}) %all-gather.3.cloned.1.call-update) | async-done | bytes 1048592 | tf_op jit(solution)/shard_map/all_gather | solution.py:36
  49.0 36.9 %conditional.1 = (f32[128,2,16]{0,2,1:T(8,128)S(1)}, f32[128,2,16,128]{0,3,2,1:T(8,128)}) conditional(s32[]{:T(128)} %convert_element_type.61, () %tuple.16, (s32[1024]{0:T(1024)S(1)}, s32[128]{0:T(128)S(1)}, s32[128]{0:T(128)S(1)}, s32[128]{0:T(128)S(1)}, s32[1024]{0:T(1024)S(1)}, /*index=5*/s32[128]{0:T(128)S(1)}, bf16[1024,512]{0,1:T(8,128)(2,1)}, ...), branch_computations={%region_3.4_spmd, %region_4.0_spmd} | conditional | flops 2202399232 | bytes 63548432 | solution.py:79
  49.0 0.3 compare_and_fusion
  49.4 2.1 fusion.32
  51.4 1.5 copy.65
  52.9 7.5 %fusion = (f32[128,2,16]{0,2,1:T(8,128)S(1)}, f32[2,1024,128,16]{2,1,3,0:T(8,128)}) fusion(pred[128,1024]{0,1:T(8,128)(4,1)S(1)} %compare_and_fusion, bf16[1024,2,128,1]{0,2,3,1:T(8,128)(2,1)S(1)} %bitcast.84, bf16[128,2,16,128]{3,2,1,0:T(8,128)(2,1)S(1)} %bitcast.80), kind=kOutput, calls=%fused_computation.5 | convolution fusion | flops 1086320640 | bytes 18497536 | tf_op jit(solution)/shard_map/cond/branch_1_fun/rkgd,pkd->rkgp/dot_general | solution.py:56
  60.4 10.6 %convert_reduce_fusion = f32[128,2,16]{0,2,1:T(8,128)S(1)} fusion(f32[128,2,16]{0,2,1:T(8,128)S(1)} %broadcast_maximum_fusion, f32[2,1024,128,16]{2,1,3,0:T(8,128)} %get-tuple-element.51, pred[128,1024]{0,1:T(8,128)(4,1)S(1)} %compare_and_fusion), kind=kLoop, calls=%fused_computation.9 | loop fusion | flops 25161728 | bytes 16941056 | tf_op jit(solution)/shard_map/cond/branch_1_fun/reduce_sum | solution.py:73
  71.0 12.0 %convolution_bitcast_fusion = f32[128,2,16,128]{3,0,2,1:T(8,128)} fusion(bf16[1024,2,128,1]{0,2,3,1:T(8,128)(2,1)} %bitcast.86, f32[2,1024,128,16]{2,1,3,0:T(8,128)} %get-tuple-element.51, f32[128,2,16]{0,2,1:T(8,128)S(1)} %broadcast_maximum_fusion, pred[128,1024]{0,1:T(8,128)(4,1)S(1)} %compare_and_fusion), kind=kOutput, calls=%fused_computation.10 | convolution fusion | flops 1090519040 | bytes 19546112 | tf_op jit(solution)/shard_map/cond/branch_1_fun/rkgp,pkd->rkgd/dot_general | solution.py:74
  83.0 2.9 copy.64
  86.0 2.9 divide_convert_fusion
  88.8 187.5 %all-gather.5.cloned.1.call-done = bf16[4096,2048]{1,0:T(8,128)(2,1)} async-done(((bf16[4096,256]{1,0:T(8,128)(2,1)}), bf16[4096,2048]{1,0:T(8,128)(2,1)}) %all-gather.5.cloned.1.call-update) | async-done | bytes 16777232 | tf_op jit(solution)/shard_map/all_gather | solution.py:111
  276.3 0.0 copy-start.4
  276.3 0.0 copy-start.6
  276.3 9.3 %convolution_convert_fusion.1 = bf16[128,2048]{1,0:T(8,128)(2,1)} fusion(bf16[128,4096]{0,1:T(8,128)(2,1)} %bitcast.79, bf16[4096,2048]{1,0:T(8,128)(2,1)} %all-gather.5.cloned.1.call-done), kind=kOutput, calls=%fused_computation.26 | convolution fusion | flops 2147745792 | bytes 18350080 | tf_op jit(solution)/shard_map/dot_general | solution.py:109
  285.6 0.0 reduce-scatter.2.cloned.1.call-update
  285.6 0.0 copy-done.4
  285.6 0.1 copy.53
  285.7 0.1 eq.42
  285.8 0.1 eq.46
  285.9 0.1 copy.52
  286.0 0.1 mul.66
  286.1 1.2 reduce-window.6
  287.2 0.2 slice_reduce_fusion
  287.5 0.0 copy-done.6
  287.5 0.1 fusion.27
  287.6 8.3 %reduce-scatter.2.cloned.1.call-done = bf16[64,2048]{1,0:T(8,128)(2,1)} async-done(((bf16[128,2048]{1,0:T(8,128)(2,1)}), bf16[64,2048]{1,0:T(8,128)(2,1)}) %reduce-scatter.2.cloned.1.call-update) | async-done | bytes 262160 | tf_op jit(solution)/shard_map/reduce_scatter | solution.py:114
  295.9 1.1 add_convert_fusion
  297.0 0.0 copy-start.3
  297.0 0.2 fusion.23
  297.2 0.8 fusion.25
  298.0 6.1 %scatter_custom_fusion = bf16[768,2048]{1,0:T(8,128)(2,1)} fusion(s32[512]{0:T(512)S(1)} %bitcast.87, bf16[]{:T(256)} %constant.60.clone.1, bf16[64,2048]{1,0:T(8,128)(2,1)} %fusion.25), kind=kCustom, calls=%fused_computation.28 | custom fusion | bytes 3407874 | tf_op jit(solution)/shard_map/scatter | solution.py:131
  304.1 0.0 copy-start.7
  304.1 75.8 %all_to_all.10 = bf16[16,48,2048]{2,1,0:T(8,128)(2,1)S(1)} all-to-all(bf16[16,48,2048]{2,1,0:T(8,128)(2,1)} %bitcast.78), channel_id=1, replica_groups=mesh['groups'=2,'sect'=8,'head'=2] {'sect','head'}, dimensions={0} | all-to-all | bytes 6291456 | tf_op jit(solution)/shard_map/all_to_all | solution.py:134
  379.9 0.0 copy-done.3
  379.9 0.0 copy-start.2
  379.9 1.7 copy-done.2
  381.6 0.0 copy-done.7
  381.6 4.0 fusion.11
  385.6 0.0 copy-done
  385.6 11.0 %convolution_convert_fusion = bf16[768,2048]{1,0:T(8,128)(2,1)} fusion(bf16[1,768,2048]{2,1,0:T(8,128)(2,1)S(1)} %copy-done, f32[768,768]{1,0:T(8,128)} %fusion.11, bf16[768,2048]{1,0:T(8,128)(2,1)} %bitcast.83, bf16[1,2048,768]{2,1,0:T(8,128)(2,1)} %param.23), kind=kOutput, calls=%fused_computation.20 | convolution fusion | flops 4836950016 | bytes 14942208 | tf_op jit(solution)/shard_map/dot_general | solution.py:139
  396.6 0.0 copy-start.5
  396.6 5.2 %all-to-all-start.1 = ((bf16[16,48,2048]{2,1,0:T(8,128)(2,1)}), bf16[16,48,2048]{2,1,0:T(8,128)(2,1)}, u32[]{:S(2)}, u32[]{:S(2)}) async-start(bf16[16,48,2048]{2,1,0:T(8,128)(2,1)} %bitcast.81), calls=%async_computation.2 | async-start | bytes 6291456 | tf_op jit(solution)/shard_map/all_to_all | solution.py:143
  401.9 0.0 copy-done.5
  401.9 0.1 copy.51
  402.0 69.9 %all-to-all-done.1 = bf16[16,48,2048]{2,1,0:T(8,128)(2,1)} async-done(((bf16[16,48,2048]{2,1,0:T(8,128)(2,1)}), bf16[16,48,2048]{2,1,0:T(8,128)(2,1)}, u32[]{:S(2)}, u32[]{:S(2)}) %all-to-all-start.1) | async-done | bytes 3145760 | tf_op jit(solution)/shard_map/all_to_all | solution.py:143
  471.9 7.6 %gather_fusion.1 = bf16[512,2048]{1,0:T(8,128)(2,1)} fusion(bf16[768,2048]{1,0:T(8,128)(2,1)} %bitcast.18, s32[1024]{0:T(1024)S(1)} %pad_clamp_fusion), kind=kCustom, calls=%fused_computation.1 | custom fusion | bytes 4196352 | tf_op jit(solution)/shard_map/gather | solution.py:147
  479.4 4.1 fusion.9
  (17 shorter events, 0.1 us)
Async XLA Ops:
  7.2 378.5 %copy-start = (bf16[1,768,2048]{2,1,0:T(8,128)(2,1)S(1)}, bf16[1,768,2048]{2,1,0:T(8,128)(2,1)}, u32[]{:S(2)}) copy-start(bf16[1,768,2048]{2,1,0:T(8,128)(2,1)} %param.25) | copy-start | bytes 9437188
  7.2 6.6 %copy-start.1 = (s32[1024]{0:T(1024)S(1)}, s32[1024]{0:T(1024)}, u32[]{:S(2)}) copy-start(s32[1024]{0:T(1024)} %param.17) | copy-start | bytes 12292
  7.2 41.8 %all-gather.3.cloned.1.call-start = ((), (), s32[]{:S(2)}) async-start(), calls=%async_computation.3 | async-start | bytes 1179648 | tf_op jit(solution)/shard_map/all_gather | solution.py:36
  10.0 266.3 %all-gather.5.cloned.1.call-start = ((), (), s32[]{:S(2)}) async-start(), calls=%async_computation.4 | async-start | bytes 18874368 | tf_op jit(solution)/shard_map/all_gather | solution.py:111
  10.8 285.1 %reduce-scatter.2.cloned.1.call-start = ((), (), s32[]{:S(2)}) async-start(), calls=%async_computation.5 | async-start | bytes 786432 | tf_op jit(solution)/shard_map/reduce_scatter | solution.py:114
  276.3 9.3 %copy-start.4 = (s32[64,8]{0,1:T(8,128)S(1)}, s32[64,8]{0,1:T(8,128)}, u32[]{:S(2)}) copy-start(s32[64,8]{0,1:T(8,128)} %param.21) | copy-start | bytes 6148
  276.3 11.2 %copy-start.6 = (bf16[2048]{0:T(1024)(128)(2,1)S(1)}, bf16[2048]{0:T(1024)(128)(2,1)}, u32[]{:S(2)}) copy-start(bf16[2048]{0:T(1024)(128)(2,1)} %param.20) | copy-start | bytes 12292
  297.0 82.9 %copy-start.3 = (bf16[64,2048]{1,0:T(8,128)(2,1)}, bf16[64,2048]{1,0:T(8,128)(2,1)S(1)}, u32[]{:S(2)}) copy-start(bf16[64,2048]{1,0:T(8,128)(2,1)S(1)} %add_convert_fusion) | copy-start | bytes 786436
  304.1 77.5 %copy-start.7 = (bf16[1,2048,768]{2,1,0:T(8,128)(2,1)S(1)}, bf16[1,2048,768]{2,1,0:T(8,128)(2,1)}, u32[]{:S(2)}) copy-start(bf16[1,2048,768]{2,1,0:T(8,128)(2,1)} %param.24) | copy-start | bytes 9437188
  379.9 1.7 copy-start.2
  396.6 5.2 %copy-start.5 = (f32[64,8]{0,1:T(8,128)S(1)}, f32[64,8]{0,1:T(8,128)}, u32[]{:S(2)}) copy-start(f32[64,8]{0,1:T(8,128)} %param.22) | copy-start | bytes 6148
  396.6 75.2 %all-to-all-start.1 = ((bf16[16,48,2048]{2,1,0:T(8,128)(2,1)}), bf16[16,48,2048]{2,1,0:T(8,128)(2,1)}, u32[]{:S(2)}, u32[]{:S(2)}) async-start(bf16[16,48,2048]{2,1,0:T(8,128)(2,1)} %bitcast.81), calls=%async_computation.2 | async-start | bytes 6291456 | tf_op jit(solution)/shard_map/all_to_all | solution.py:143
Sparse Core Ops, SparseCore 0:
  10.6 38.3 all-gather.2
  51.0 225.1 all-gather.4
  285.7 10.1 reduce-scatter.1
